TPU v7x, 128 devices: a whole 4x4x4 slice. The times are simulated.
128 devices in a mesh: blk: 16 (over z, y), beam: 8 (over x, core).
Axes of the slice: x: 4, y: 4, z: 4, core: 2. Of those that a mesh axis runs over, the one named last changes fastest.
Arguments:
- sky_coefficients: bfloat16 [2, 128, 3, 2, 32, 4096], P(None, None, None, None, 'blk'), may hold values from -6 to 6
- beam_window: bfloat16 [2, 16, 4096], P(None, 'beam'), may hold values from -5 to 5
- legendre: bfloat16 [32, 2, 4096, 256], P('blk'), as said below
- azimuth_modes: int32 [32], P('blk'), may hold values from 0 to 8191, as said below
- orientation: float32 [128, 16, 512], P('beam'), may hold values from -1 to 1
Outputs:
- sky_map: bfloat16 [128, 3, 512, 128], P('beam', None, 'blk')
Inputs may be any that keep to these rules, and one draw needn't show every extreme that they name: `azimuth_modes`: distinct values; 0 and 8191 are always among them. legendre[m, p, i, t] is zero wherever 2 * i + p < azimuth_modes[m].
All inputs are finite; a program needn't handle non-finite values.
Results may differ from a plain program's by a relative error of at most 0.0049.
Values may be sent and summed in bfloat16 or wider, within the bound.
No kernel may reach another device: no remote copies, remote signals or barrier semaphores. Data moves between devices by JAX's collectives and lax.ppermute only.
A program may use at most 256 MiB of HBM per device.

v0:
```python
import math

import jax
import jax.numpy as jnp
from jax import lax
from jax.experimental import pallas as pl
from jax.experimental.layout import Layout, with_layout_constraint
from jax.experimental.pallas import tpu as pltpu
from jax.sharding import PartitionSpec as P

LMAX = 8192
NPHI = 128
CHUNK = 1024
TILES = CHUNK // 128
BF = jnp.bfloat16
F32 = jnp.float32


def mirror():
    lane = lax.broadcasted_iota(jnp.int32, (256, 256), 0)
    return jnp.where(lane + lax.broadcasted_iota(jnp.int32, (256, 256), 1) == 255, 1.0, 0.0).astype(BF)


def chunk_at(c):
    return pl.ds(pl.multiple_of(c * CHUNK, CHUNK), CHUNK)


def first_chunk(modes, slot, p, chunks):
    return jnp.minimum((modes[slot] - p + 1) // 2 // CHUNK, chunks - 1)


def weighted(lines, win, bases, tiles):
    parts = []
    for base in bases:
        gain = [jnp.broadcast_to(win[pl.ds(base + 2 * i, 1), :], (16, 128)).astype(BF) for i in range(tiles)]
        gain = jnp.concatenate(gain, 1)
        parts += [line * gain for line in lines]
    return jnp.concatenate(parts, 0)


def sky_lines(coef, slot, p, tile, tiles):
    return [
        jnp.concatenate([coef[slot, p, j // 2, tile + i, pl.ds(j % 2 * 16, 16), :] for i in range(tiles)], 1)
        for j in range(6)
    ]


def orient(start, spins, acc, components):
    north, south = [None] * 12, [None] * 12
    for h in range(2):
        n = [None if start is None else start[0, pl.ds(cr * 16 + h * 8, 8), :] for cr in range(6)]
        s = [None if start is None else start[1, pl.ds(cr * 16 + h * 8, 8), :] for cr in range(6)]
        for at, k in enumerate(components):
            spin = spins[k, pl.ds(h * 8, 8), :]
            for cr in range(6):
                rows = pl.ds(at * 96 + cr * 16 + h * 8, 8)
                even, odd = acc[0, rows, :], acc[1, rows, :]
                up = (even + odd) * spin[:, :256]
                down = (even - odd) * spin[:, 256:]
                n[cr] = up if n[cr] is None else n[cr] + up
                s[cr] = down if s[cr] is None else s[cr] + down
        for cr in range(6):
            north[2 * cr + h] = n[cr]
            south[2 * cr + h] = s[cr]
    return jnp.concatenate(north, 0), jnp.concatenate(south, 0)


def begin_kernel(
    me, modes_in, sky, orient_in, window, table, coef_out, weights, tail, partial, lead_coef, lead_leg,
    modes, raw, turns, own, win, leg, acc, wide, lines, coef, sems, leg_sems, sky_sems, coef_sems, lead_sems,
):
    mine = me[0]
    chunks = table.shape[2] // CHUNK
    rows = sky.shape[4]
    pitch = 2 * rows + 4
    fetch_modes = pltpu.make_async_copy(modes_in, modes, sems.at[0])
    fetch_orient = pltpu.make_async_copy(orient_in, turns, sems.at[1])
    fetch_window = pltpu.make_async_copy(window, own, sems.at[2])
    fetch_modes.start()

    def sky_copy(p, c):
        return pltpu.make_async_copy(sky.at[p, pl.ds(mine * 16, 16), c], raw.at[p, c], sky_sems.at[p, c])

    fetch_orient.start()
    for p in range(2):
        for c in range(3):
            sky_copy(p, c).start()
    fetch_window.start()
    fetch_modes.wait()

    def leg_copy(slot, p, c):
        at = chunk_at(c)
        return pltpu.make_async_copy(table.at[slot, p, at, :], leg.at[slot, p, at, :], leg_sems.at[slot, p, c])

    for slot in range(2):
        for p in range(2):
            lax.fori_loop(
                first_chunk(modes, slot, p, chunks), chunks, lambda c, _: (leg_copy(slot, p, c).start(), 0)[1], 0
            )

    row = lax.broadcasted_iota(jnp.int32, (8, 128), 0)
    mode = jnp.where(row < 4, modes[0], modes[1])
    column = lax.broadcasted_iota(jnp.int32, (8, 128), 1)
    phase = ((mode * column) % (2 * LMAX)).astype(F32) * (math.pi / LMAX)
    weight = jnp.where(mode == 0, 1.0, 2.0)
    basis = jnp.where(row % 4 < 2, weight * jnp.cos(phase), -weight * jnp.sin(phase))
    high = basis.astype(BF).astype(F32)
    tail[...] = jnp.where(row % 2 == 0, high, basis - high).astype(BF)

    fetch_orient.wait()
    flip = mirror()
    for t in range(4):
        for s in range(16):
            lines[pl.ds(320 * t + 20 * s, 16), :] = turns[pl.ds(16 * s, 16), pl.ds(128 * t, 128)]

    def pick(k, t):
        return lines[pl.ds(320 * t + k, 16, stride=20), :]

    for k in range(16):
        weights[k, :, pl.ds(0, 256)] = jnp.concatenate([pick(k, 0), pick(k, 1)], 1)
    south = jnp.concatenate([jnp.concatenate([pick(k, 2), pick(k, 3)], 1) for k in range(16)], 0)
    total = jnp.zeros((256, 256), F32)
    for _ in range(3):
        piece = south.astype(BF)
        total = total + jnp.dot(piece, flip, preferred_element_type=F32)
        south = south - piece.astype(F32)
    weights[:, :, pl.ds(256, 256)] = total.reshape(16, 16, 256)

    def coef_copy(m, p, c):
        return pltpu.make_async_copy(coef.at[m, p, c], coef_out.at[m, p, c], coef_sems.at[m, p, c])

    def arrange(p, c):
        sky_copy(p, c).wait()
        for s in range(16):
            wide[pl.ds(s * pitch, 2 * rows), :] = raw[p, c, s].reshape(2 * rows, 128).astype(F32)
        for r in range(2):
            for row in range(rows):
                line = wide[pl.ds(r * rows + row, 16, stride=pitch), :].astype(BF)
                coef[row % 2, p, c, row // 2, pl.ds(r * 16, 16), :] = line
        for m in range(2):
            coef_copy(m, p, c).start()

    for p in range(2):
        for c in range(3):
            arrange(p, c)

    def lead_copies():
        c = first_chunk(modes, 0, 0, chunks)
        its = pl.ds(pl.multiple_of(c * TILES, TILES), TILES)
        return (
            pltpu.make_async_copy(coef.at[0, 0, :, its], lead_coef, lead_sems.at[0]),
            pltpu.make_async_copy(leg.at[0, 0, chunk_at(c), :], lead_leg, lead_sems.at[1]),
        )

    fetch_window.wait()
    win[...] = own[...].astype(F32).reshape(win.shape)
    for slot in range(2):
        for p in range(2):

            def body(c, _, slot=slot, p=p):
                leg_copy(slot, p, c).wait()
                base = p * (2 * TILES * chunks) + c * (2 * TILES)
                tile = pl.multiple_of(c * TILES, TILES)
                lhs = weighted(sky_lines(coef, slot, p, tile, TILES), win, [base, base + 1], TILES)
                part = jnp.dot(lhs, leg[slot, p, chunk_at(c), :], preferred_element_type=F32)
                acc[p] = jnp.where(c == first_chunk(modes, slot, p, chunks), 0.0, acc[p]) + part
                return 0

            lax.fori_loop(first_chunk(modes, slot, p, chunks), chunks, body, 0)
        if slot == 0:
            for copy in lead_copies():
                copy.start()
        partial[slot, 0], partial[slot, 1] = orient(None, weights, acc, [2 * mine, 2 * mine + 1])
    for copy in lead_copies():
        copy.wait()
    for m in range(2):
        for p in range(2):
            for c in range(3):
                coef_copy(m, p, c).wait()


def begin(me, modes, sky, orient, window, table):
    half = table.shape[2]
    tiles = half // 128
    vm = pl.BlockSpec(memory_space=pltpu.VMEM)
    hbm = pl.BlockSpec(memory_space=pltpu.HBM)
    return pl.pallas_call(
        begin_kernel,
        out_shape=(
            pltpu.HBM((2, 2, 3, tiles, 32, 128), BF),
            jax.ShapeDtypeStruct((16, 16, 512), F32),
            jax.ShapeDtypeStruct((8, 128), BF),
            jax.ShapeDtypeStruct((2, 2, 96, 256), F32),
            jax.ShapeDtypeStruct((3, TILES, 32, 128), BF),
            jax.ShapeDtypeStruct((CHUNK, 256), BF),
        ),
        in_specs=[pl.BlockSpec(memory_space=pltpu.SMEM), hbm, hbm, hbm, hbm, hbm],
        out_specs=(hbm, vm, vm, vm, vm, vm),
        scratch_shapes=[
            pltpu.SMEM((2,), jnp.int32),
            pltpu.VMEM((2, 3, 16, 2, 2 * tiles, 128), BF),
            pltpu.VMEM((256, 512), F32),
            pltpu.VMEM(window.shape, BF),
            pltpu.VMEM((4 * tiles, 128), F32),
            pltpu.VMEM(table.shape, BF),
            pltpu.VMEM((2, 192, 256), F32),
            pltpu.VMEM((64 * tiles + 64, 128), F32),
            pltpu.VMEM((1280, 128), F32),
            pltpu.VMEM((2, 2, 3, tiles, 32, 128), BF),
            pltpu.SemaphoreType.DMA((3,)),
            pltpu.SemaphoreType.DMA((2, 2, half // CHUNK)),
            pltpu.SemaphoreType.DMA((2, 3)),
            pltpu.SemaphoreType.DMA((2, 2, 3)),
            pltpu.SemaphoreType.DMA((2,)),
        ],
        compiler_params=pltpu.CompilerParams(vmem_limit_bytes=30 * 2**20),
        cost_estimate=pl.CostEstimate(flops=4 * 10**9, bytes_accessed=16 * 10**6, transcendentals=0),
        name="begin",
    )(me, modes, sky, orient, window, table)


def synth_kernel(
    me, modes, coef_in, window, table, weights, tail, partial, lead_coef, lead_leg,
    out, coef, leg, acc, win, maps, sems, coef_sems,
):
    mine = me[0]
    halves = table.shape[2] // CHUNK * 2
    others = [(mine + 1 + j) % 8 for j in range(7)]

    def span(slot, p):
        count = halves - jnp.minimum((modes[slot] - p + 1) // 2 // (CHUNK // 2), halves - 1)
        return (halves - count + 1) // 2, count % 2 == 1

    def copies(slot, p, c, tile, tiles):
        at = pl.ds(pl.multiple_of(tile * 128, tiles * 128), tiles * 128)
        its = pl.ds(pl.multiple_of(tile, tiles), tiles)
        return (
            pltpu.make_async_copy(
                coef_in.at[slot, p, :, its], coef.at[slot, p, :, its], coef_sems.at[slot, p, c]
            ),
            pltpu.make_async_copy(table.at[slot, p, at, :], leg.at[slot, p, at, :], sems.at[slot, p, c]),
        )

    def whole(c):
        return c, c * TILES, TILES

    def part(c):
        return c - 1, c * TILES - TILES // 2, TILES // 2

    def fetch(slot, p, where):
        for copy in copies(slot, p, *where):
            copy.start()

    def lead(at, tile, tiles):
        to = pl.ds(pl.multiple_of(tile * 128, tiles * 128), tiles * 128)
        its = pl.ds(pl.multiple_of(tile, tiles), tiles)
        c = tile // TILES
        return (
            pltpu.make_async_copy(lead_coef.at[:, pl.ds(at, tiles)], coef.at[0, 0, :, its], coef_sems.at[0, 0, c]),
            pltpu.make_async_copy(lead_leg.at[pl.ds(at * 128, tiles * 128)], leg.at[0, 0, to, :], sems.at[0, 0, c]),
        )

    def fetch_lead(at, where):
        for copy in lead(at, *where[1:]):
            copy.start()

    for slot in range(2):
        for p in range(2):
            start, half = span(slot, p)
            rest = start
            if slot == 0 and p == 0:

                @pl.when(half)
                def _(start=start):
                    fetch_lead(TILES // 2, part(start))

                @pl.when(jnp.logical_not(half))
                def _(start=start):
                    fetch_lead(0, whole(start))

                rest = jnp.where(half, start, start + 1)
            else:

                @pl.when(half)
                def _(slot=slot, p=p, start=start):
                    fetch(slot, p, part(start))

            lax.fori_loop(rest, halves // 2, lambda c, _: (fetch(slot, p, whole(c)), 0)[1], 0)
    win[...] = window[...].astype(F32).reshape(win.shape)

    def step(slot, p, c, tile, tiles):
        for copy in copies(slot, p, c, tile, tiles):
            copy.wait()
        tile = pl.multiple_of(tile, tiles)
        at = pl.ds(pl.multiple_of(tile * 128, tiles * 128), tiles * 128)
        bases = [(src * 2 + p) * (halves * TILES) + 2 * tile + kk for src in others for kk in range(2)]
        lhs = weighted(sky_lines(coef, slot, p, tile, tiles), win, bases, tiles)
        return jnp.dot(lhs, leg[slot, p, at, :], preferred_element_type=F32)

    for dst in range(16):
        out[dst, pl.ds(48, 8), :] = tail[...]
    for slot in range(2):
        for p in range(2):
            start, half = span(slot, p)

            @pl.when(half)
            def _(slot=slot, p=p, start=start):
                acc[slot, p] = step(slot, p, *part(start))

            fresh = jnp.where(half, -1, start)

            def body(c, _, slot=slot, p=p, fresh=fresh):
                more = step(slot, p, *whole(c))
                acc[slot, p] = jnp.where(c == fresh, 0.0, acc[slot, p]) + more
                return 0

            lax.fori_loop(start, halves // 2, body, 0)

    flip = mirror()
    group = lax.broadcasted_iota(jnp.int32, (24, 128), 1) // 32
    components = [2 * src + kk for src in others for kk in range(2)]
    for slot in range(2):
        sign = jnp.where(modes[slot] % 2 == 0, 1.0, -1.0).astype(F32)
        north, south = orient(partial.at[slot], weights, acc.at[slot], components)
        south = jnp.dot((south * sign).astype(BF), flip, preferred_element_type=F32)
        for tile in range(4):
            hemisphere = north if tile < 2 else south
            maps[slot, tile] = hemisphere[:, tile % 2 * 128:tile % 2 * 128 + 128]
    for slot in range(2):
        for tile in range(4):
            pieces = [maps[slot, tile, pl.ds(b, 24, stride=4), :] for b in range(4)]
            for g in range(4):
                send = pieces[g]
                for b in range(4):
                    if b != g:
                        send = jnp.where(group == b, pltpu.roll(pieces[b], ((b - g) * 32) % 128, 1), send)
                out[tile * 4 + g, pl.ds(slot * 24, 24), :] = send.astype(BF)


def synth(me, modes, coef, window, table, *rest):
    half = table.shape[2]
    vm = pl.BlockSpec(memory_space=pltpu.VMEM)
    smem = pl.BlockSpec(memory_space=pltpu.SMEM)
    hbm = pl.BlockSpec(memory_space=pltpu.HBM)
    return pl.pallas_call(
        synth_kernel,
        out_shape=jax.ShapeDtypeStruct((16, 56, 128), BF),
        in_specs=[smem, smem, hbm, vm, hbm, vm, vm, vm, vm, vm],
        out_specs=vm,
        scratch_shapes=[
            pltpu.VMEM(coef.shape, BF),
            pltpu.VMEM(table.shape, BF),
            pltpu.VMEM((2, 2, 1344, 256), F32),
            pltpu.VMEM((window.shape[0] * half // 32, 128), F32),
            pltpu.VMEM((2, 4, 96, 128), F32),
            pltpu.SemaphoreType.DMA((2, 2, half // CHUNK)),
            pltpu.SemaphoreType.DMA((2, 2, half // CHUNK)),
        ],
        compiler_params=pltpu.CompilerParams(vmem_limit_bytes=26 * 2**20),
        cost_estimate=pl.CostEstimate(flops=12 * 10**9, bytes_accessed=12 * 10**6, transcendentals=0),
        name="synth",
    )(me, modes, coef, window, table, *rest)


def map_kernel(got, out, wide, held, sems):
    for src in range(16):
        wide[pl.ds(src * 60, 56), :] = got[src].astype(F32)

    def take(row):
        return wide[pl.ds(row, 16, stride=60), :]

    basis = [take(48 + slot * 4 + r * 2 + part) for part in range(2) for r in range(2) for slot in range(2)]
    basis = jnp.concatenate(basis, 0).astype(BF)
    for c in range(3):
        for a in range(4):
            x = jnp.concatenate([take(slot * 24 + c * 8 + r * 4 + a) for r in range(2) for slot in range(2)], 0)
            x = x.T.astype(BF)
            y = jnp.dot(jnp.concatenate([x, x], 1), basis, preferred_element_type=F32)
            for b in range(4):
                held[c, 4 * a + b] = y[b * 32:(b + 1) * 32].astype(BF)
        pltpu.make_async_copy(held.at[c], out.at[:, c], sems.at[c]).start()
    for c in range(3):
        pltpu.make_async_copy(held.at[c], out.at[:, c], sems.at[c]).wait()


def to_map(got):
    vm = pl.BlockSpec(memory_space=pltpu.VMEM)
    return pl.pallas_call(
        map_kernel,
        out_shape=pltpu.HBM((16, 3, 32, NPHI), BF),
        in_specs=[vm],
        out_specs=pl.BlockSpec(memory_space=pltpu.HBM),
        scratch_shapes=[
            pltpu.VMEM((16 * 60, 128), F32),
            pltpu.VMEM((3, 16, 32, NPHI), BF),
            pltpu.SemaphoreType.DMA((3,)),
        ],
        compiler_params=pltpu.CompilerParams(vmem_limit_bytes=6 * 2**20),
        name="to_map",
    )(got)


def paired(x):
    lead = x.shape[:-2]
    x = x.reshape(lead + (2, x.shape[-1] // 128, 128))
    return jnp.swapaxes(x, -3, -2).reshape(lead + (-1, 128))


def rowwise(x):
    return with_layout_constraint(x, Layout(major_to_minor=tuple(range(x.ndim))))


def shards(sky_coefficients, beam_window, legendre, azimuth_modes, orientation):
    me = lax.axis_index("beam").astype(jnp.int32)[None]
    def stay(x):
        return pltpu.with_memory_space_constraint(x, pltpu.HBM)

    own = stay(paired(beam_window))
    legendre = stay(legendre)
    window = lax.all_to_all(jnp.broadcast_to(rowwise(paired(beam_window))[None], (8,) + own.shape), "beam", 0, 0, tiled=True)
    coef, *rest = begin(
        me, stay(azimuth_modes), stay(paired(sky_coefficients)), stay(orientation.reshape(256, 512)), own, legendre
    )
    sent = synth(me, azimuth_modes, stay(coef), window, legendre, *rest)
    got = lax.all_to_all(sent, "blk", 0, 0, tiled=True)
    return to_map(got)


def solution(mesh):
    placed = (
        P(None, None, None, None, "blk", None),
        P(None, "beam", None),
        P("blk", None, None, None),
        P("blk"),
        P("beam", None, None),
    )
    return jax.shard_map(
        shards, mesh=mesh, in_specs=placed, out_specs=P("beam", None, "blk", None), check_vma=False
    )
```

profile of v0, /device:TPU:1, one launch (start us, length us, event | category | flops | bytes accessed | tf_op | source)
XLA Modules:
  0.0 45.3 jit_solution(6823897193941109914)
XLA Ops:
  0.0 1.5 %broadcast_in_dim.10 = bf16[8,2,64,128]{3,2,1,0:T(8,128)(2,1)} broadcast(bf16[2,64,128]{2,1,0:T(8,128)(2,1)} %bitcast.14), dimensions={1,2,3} | broadcast | bytes 294912 | tf_op jit(solution)/shard_map/broadcast_in_dim | solution.py:420
  1.5 5.8 %all-to-all-start = ((bf16[8,2,64,128]{3,2,1,0:T(8,128)(2,1)}), bf16[8,2,64,128]{3,2,1,0:T(8,128)(2,1)S(1)}, u32[]{:S(2)}, u32[]{:S(2)}) async-start(bf16[8,2,64,128]{3,2,1,0:T(8,128)(2,1)} %broadcast_in_dim.10), calls=%async_computation | async-start | bytes 524288 | tf_op jit(solution)/shard_map/all_to_all | solution.py:420
  7.3 0.0 copy-start
  7.3 6.1 %begin.1 = (bf16[2,2,3,32,32,128]{5,4,3,2,1,0:T(8,128)(2,1)}, f32[16,16,512]{2,1,0:T(8,128)S(1)}, bf16[8,128]{1,0:T(8,128)(2,1)S(1)}, f32[2,2,96,256]{3,2,1,0:T(...) custom-call(s32[1]{0:T(128)} %bitcast.me, s32[2]{0:T(128)} %modes.1, ...), custom_call_target="tpu_custom_call" | custom-call | flops 4000000000 | bytes 16000000 | tf_op jit(solution)/shard_map/begin/pallas_call | solution.py:187
  13.4 0.4 all-to-all-done.window
  13.8 0.0 copy-done
  13.8 10.0 %synth.1 = bf16[16,56,128]{2,1,0:T(8,128)(2,1)S(1)} custom-call(s32[1]{0:T(128)} %bitcast.me, s32[2]{0:T(128)S(1)} %copy-done, bf16[2,2,3,32,32,128]{5,4,3,2,1,0:T(8,128)(2,1)} %get-tuple-element.11.coef_in, bf16[8,2,64,128]{3,2,1,0:T(8,128)(2,1)S(1)} %all-to-all-done.window, bf16[2,2,4096,256]{3,2,1,0:T(8,128)(2,1)} %table.3, ...), custom_call_target="tpu_custom_call" | custom-call | flops 12000000000 | bytes 12000000 | tf_op jit(solution)/shard_map/synth/pallas_call | solution.py:345
  23.8 20.2 %all_to_all.10.got = bf16[16,56,128]{2,1,0:T(8,128)(2,1)S(1)} all-to-all(bf16[16,56,128]{2,1,0:T(8,128)(2,1)S(1)} %synth.1), channel_id=1, replica_groups=mesh['blk'=16,'beam'=8] {'blk'}, dimensions={0} | all-to-all | bytes 458752 | tf_op jit(solution)/shard_map/all_to_all | solution.py:425
  44.0 1.2 %to_map.1 = bf16[16,3,32,128]{3,2,1,0:T(8,128)(2,1)} custom-call(bf16[16,56,128]{2,1,0:T(8,128)(2,1)S(1)} %all_to_all.10.got), custom_call_target="tpu_custom_call" | custom-call | tf_op jit(solution)/shard_map/to_map/pallas_call | solution.py:388
Async XLA Ops:
  1.5 12.3 %all-to-all-start = ((bf16[8,2,64,128]{3,2,1,0:T(8,128)(2,1)}), bf16[8,2,64,128]{3,2,1,0:T(8,128)(2,1)S(1)}, u32[]{:S(2)}, u32[]{:S(2)}) async-start(bf16[8,2,64,128]{3,2,1,0:T(8,128)(2,1)} %broadcast_in_dim.10), calls=%async_computation | async-start | bytes 524288 | tf_op jit(solution)/shard_map/all_to_all | solution.py:420
  7.3 6.5 %copy-start = (s32[2]{0:T(128)S(1)}, s32[2]{0:T(128)}, u32[]{:S(2)}) copy-start(s32[2]{0:T(128)} %modes.1) | copy-start | bytes 28
where the time goes:
time: 46.1 us; the launch traced here: 45.3 us
  blocking collectives  20.2 us (44%)
  Pallas kernels  17.3 us (38%)
  starting transfers between devices  5.79 us (13%)
  local copies, waits for them, and re-layouts  1.51 us (3%)
    all_to_all x1, blocking collectives, shards(): got = lax.all_to_all(sent, 'blk', 0, 0, tiled=True)  20.2 us
    pallas_call x1, Pallas kernels, synth(): pl.pallas_call(synth_kernel, out_shape=jax.ShapeDtypeStruct((16, 56, 128)...  10 us
    pallas_call x1, Pallas kernels, begin(): pl.pallas_call(begin_kernel, out_shape=(pltpu.HBM((2, 2, 3, tiles, 32, 12...  6.1 us
    all_to_all x1, starting transfers between devices, shards(): lax.all_to_all(jnp.broadcast_to(rowwise(paired(beam_window))[None], (8,)...  5.79 us
    broadcast_in_dim x1, local copies, waits for them, and re-layouts, shards(): jnp.broadcast_to(rowwise(paired(beam_window))[None], (8,) + own.shape)  1.51 us
    pallas_call x1, Pallas kernels, to_map(): pl.pallas_call(map_kernel, out_shape=pltpu.HBM((16, 3, 32, NPHI), BF), in...  1.21 us
  transfers between devices with their start and end apart: 1, of which 1 were waited for; matrix products, arithmetic and copies ran while one was open for 0% of the time, Pallas kernels for 13%

commit v1 on v0

--- a/solution.py
+++ b/solution.py
@@ -12,6 +12,7 @@
 NPHI = 128
 CHUNK = 1024
 TILES = CHUNK // 128
+SHIFT = CHUNK.bit_length()
 BF = jnp.bfloat16
 F32 = jnp.float32
 
@@ -26,7 +27,7 @@
 
 
 def first_chunk(modes, slot, p, chunks):
-    return jnp.minimum((modes[slot] - p + 1) // 2 // CHUNK, chunks - 1)
+    return jnp.minimum((modes[slot] + (1 - p)) >> SHIFT, chunks - 1)
 
 
 def weighted(lines, win, bases, tiles):
@@ -45,7 +46,7 @@
     ]
 
 
-def orient(start, spins, acc, components):
+def orient(start, spins, acc, components, mixed):
     north, south = [None] * 12, [None] * 12
     for h in range(2):
         n = [None if start is None else start[0, pl.ds(cr * 16 + h * 8, 8), :] for cr in range(6)]
@@ -54,9 +55,10 @@
             spin = spins[k, pl.ds(h * 8, 8), :]
             for cr in range(6):
                 rows = pl.ds(at * 96 + cr * 16 + h * 8, 8)
-                even, odd = acc[0, rows, :], acc[1, rows, :]
-                up = (even + odd) * spin[:, :256]
-                down = (even - odd) * spin[:, 256:]
+                up, down = acc[0, rows, :], acc[1, rows, :]
+                if not mixed:
+                    up, down = up + down, up - down
+                up, down = up * spin[:, :256], down * spin[:, 256:]
                 n[cr] = up if n[cr] is None else n[cr] + up
                 s[cr] = down if s[cr] is None else s[cr] + down
         for cr in range(6):
@@ -170,7 +172,7 @@
         if slot == 0:
             for copy in lead_copies():
                 copy.start()
-        partial[slot, 0], partial[slot, 1] = orient(None, weights, acc, [2 * mine, 2 * mine + 1])
+        partial[slot, 0], partial[slot, 1] = orient(None, weights, acc, [2 * mine, 2 * mine + 1], False)
     for copy in lead_copies():
         copy.wait()
     for m in range(2):
@@ -225,11 +227,11 @@
 ):
     mine = me[0]
     halves = table.shape[2] // CHUNK * 2
-    others = [(mine + 1 + j) % 8 for j in range(7)]
+    others = [(mine + 1 + j) & 7 for j in range(7)]
 
     def span(slot, p):
-        count = halves - jnp.minimum((modes[slot] - p + 1) // 2 // (CHUNK // 2), halves - 1)
-        return (halves - count + 1) // 2, count % 2 == 1
+        skip = jnp.minimum((modes[slot] + (1 - p)) >> (SHIFT - 1), halves - 1)
+        return (skip + 1) >> 1, skip & 1 == 1
 
     def copies(slot, p, c, tile, tiles):
         at = pl.ds(pl.multiple_of(tile * 128, tiles * 128), tiles * 128)
@@ -251,17 +253,16 @@
         for copy in copies(slot, p, *where):
             copy.start()
 
-    def lead(at, tile, tiles):
+    def lead(at, c, tile, tiles):
         to = pl.ds(pl.multiple_of(tile * 128, tiles * 128), tiles * 128)
         its = pl.ds(pl.multiple_of(tile, tiles), tiles)
-        c = tile // TILES
         return (
             pltpu.make_async_copy(lead_coef.at[:, pl.ds(at, tiles)], coef.at[0, 0, :, its], coef_sems.at[0, 0, c]),
             pltpu.make_async_copy(lead_leg.at[pl.ds(at * 128, tiles * 128)], leg.at[0, 0, to, :], sems.at[0, 0, c]),
         )
 
     def fetch_lead(at, where):
-        for copy in lead(at, *where[1:]):
+        for copy in lead(at, *where):
             copy.start()
 
     for slot in range(2):
@@ -303,25 +304,46 @@
         for p in range(2):
             start, half = span(slot, p)
 
-            @pl.when(half)
-            def _(slot=slot, p=p, start=start):
-                acc[slot, p] = step(slot, p, *part(start))
-
-            fresh = jnp.where(half, -1, start)
-
-            def body(c, _, slot=slot, p=p, fresh=fresh):
-                more = step(slot, p, *whole(c))
-                acc[slot, p] = jnp.where(c == fresh, 0.0, acc[slot, p]) + more
-                return 0
-
-            lax.fori_loop(start, halves // 2, body, 0)
+            if p == 0:
+
+                @pl.when(half)
+                def _(slot=slot, start=start):
+                    acc[slot, 0] = step(slot, 0, *part(start))
+
+                fresh = jnp.where(half, -1, start)
+
+                def body(c, _, slot=slot, fresh=fresh):
+                    more = step(slot, 0, *whole(c))
+                    acc[slot, 0] = jnp.where(c == fresh, 0.0, acc[slot, 0]) + more
+                    return 0
+
+                lax.fori_loop(start, halves // 2, body, 0)
+            else:
+
+                @pl.when(half)
+                def _(slot=slot, start=start):
+                    more = step(slot, 1, *part(start))
+                    both = acc[slot, 0]
+                    acc[slot, 0] = both + more
+                    acc[slot, 1] = both - more
+
+                fresh = jnp.where(half, -1, start)
+
+                def body(c, _, slot=slot, fresh=fresh):
+                    more = step(slot, 1, *whole(c))
+                    total = acc[slot, 0]
+                    acc[slot, 1] = jnp.where(c == fresh, total, acc[slot, 1]) - more
+                    acc[slot, 0] = total + more
+                    return 0
+
+                lax.fori_loop(start, halves // 2, body, 0)
 
     flip = mirror()
     group = lax.broadcasted_iota(jnp.int32, (24, 128), 1) // 32
     components = [2 * src + kk for src in others for kk in range(2)]
     for slot in range(2):
         sign = jnp.where(modes[slot] % 2 == 0, 1.0, -1.0).astype(F32)
-        north, south = orient(partial.at[slot], weights, acc.at[slot], components)
+        north, south = orient(partial.at[slot], weights, acc.at[slot], components, True)
         south = jnp.dot((south * sign).astype(BF), flip, preferred_element_type=F32)
         for tile in range(4):
             hemisphere = north if tile < 2 else south

time: 46.1 us -> 47.5 us (1.030); the launches traced: 45.3 us -> 47.5 us
  blocking collectives: 20.2 us -> 27.4 us
  Pallas kernels: 17.3 us -> 10.7 us
  waiting for transfers between devices: 0.36 us -> 2.03 us
    all_to_all x1, blocking collectives: 20.2 us -> 27.4 us  [shards(): got = lax.all_to_all(sent, 'blk', 0, 0, tiled=True)]
    pallas_call x1, Pallas kernels: 10 us -> 5.07 us  [synth(): pl.pallas_call(synth_kernel, out_shape=jax.ShapeDtypeStruct((16, 56, 128)...]
    pallas_call x1, Pallas kernels: 6.1 us -> 4.43 us  [begin(): pl.pallas_call(begin_kernel, out_shape=(pltpu.HBM((2, 2, 3, tiles, 32, 12...]
    all_to_all x1, waiting for transfers between devices: 0.36 us -> 2.03 us  [shards(): lax.all_to_all(jnp.broadcast_to(rowwise(paired(beam_window))[None], (8,)...]
  transfers between devices with their start and end apart: 1 -> 1, of which waited for: 1 -> 1; matrix products, arithmetic and copies ran while one was open for 0% -> 0% of each run, Pallas kernels for 13% -> 9%
where the time goes in v1:
time: 47.5 us
  blocking collectives  27.4 us (58%)
  Pallas kernels  10.7 us (23%)
  starting transfers between devices  5.79 us (12%)
  waiting for transfers between devices  2.03 us (4%)
  local copies, waits for them, and re-layouts  1.51 us (3%)
    all_to_all x1, blocking collectives, shards(): got = lax.all_to_all(sent, 'blk', 0, 0, tiled=True)  27.4 us
    all_to_all x1, starting transfers between devices, shards(): lax.all_to_all(jnp.broadcast_to(rowwise(paired(beam_window))[None], (8,)...  5.79 us
    pallas_call x1, Pallas kernels, synth(): pl.pallas_call(synth_kernel, out_shape=jax.ShapeDtypeStruct((16, 56, 128)...  5.07 us
    pallas_call x1, Pallas kernels, begin(): pl.pallas_call(begin_kernel, out_shape=(pltpu.HBM((2, 2, 3, tiles, 32, 12...  4.43 us
    all_to_all x1, waiting for transfers between devices, shards(): lax.all_to_all(jnp.broadcast_to(rowwise(paired(beam_window))[None], (8,)...  2.03 us
    broadcast_in_dim x1, local copies, waits for them, and re-layouts, shards(): jnp.broadcast_to(rowwise(paired(beam_window))[None], (8,) + own.shape)  1.51 us
    pallas_call x1, Pallas kernels, to_map(): pl.pallas_call(map_kernel, out_shape=pltpu.HBM((16, 3, 32, NPHI), BF), in...  1.21 us
  transfers between devices with their start and end apart: 1, of which 1 were waited for; matrix products, arithmetic and copies ran while one was open for 0% of the time, Pallas kernels for 9%

profile of v1, /device:TPU:1, one launch (start us, length us, event | category | flops | bytes accessed | tf_op | source)
XLA Modules:
  0.0 47.5 jit_solution(5713713116486147047)
XLA Ops:
  0.0 1.5 %broadcast_in_dim.10 = bf16[8,2,64,128]{3,2,1,0:T(8,128)(2,1)} broadcast(bf16[2,64,128]{2,1,0:T(8,128)(2,1)} %bitcast.14), dimensions={1,2,3} | broadcast | bytes 294912 | tf_op jit(solution)/shard_map/broadcast_in_dim | solution.py:442
  1.5 5.8 %all-to-all-start = ((bf16[8,2,64,128]{3,2,1,0:T(8,128)(2,1)}), bf16[8,2,64,128]{3,2,1,0:T(8,128)(2,1)S(1)}, u32[]{:S(2)}, u32[]{:S(2)}) async-start(bf16[8,2,64,128]{3,2,1,0:T(8,128)(2,1)} %broadcast_in_dim.10), calls=%async_computation | async-start | bytes 524288 | tf_op jit(solution)/shard_map/all_to_all | solution.py:442
  7.3 0.0 copy-start
  7.3 4.4 %begin.1 = (bf16[2,2,3,32,32,128]{5,4,3,2,1,0:T(8,128)(2,1)}, f32[16,16,512]{2,1,0:T(8,128)S(1)}, bf16[8,128]{1,0:T(8,128)(2,1)S(1)}, f32[2,2,96,256]{3,2,1,0:T(...) custom-call(s32[1]{0:T(128)} %bitcast.me, s32[2]{0:T(128)} %modes.1, ...), custom_call_target="tpu_custom_call" | custom-call | flops 4000000000 | bytes 16000000 | tf_op jit(solution)/shard_map/begin/pallas_call | solution.py:189
  11.7 2.0 %all-to-all-done.window = bf16[8,2,64,128]{3,2,1,0:T(8,128)(2,1)S(1)} async-done(((bf16[8,2,64,128]{3,2,1,0:T(8,128)(2,1)}), bf16[8,2,64,128]{3,2,1,0:T(8,128)(2,1)S(1)}, u32[]{:S(2)}, u32[]{:S(2)}) %all-to-all-start) | async-done | bytes 262176 | tf_op jit(solution)/shard_map/all_to_all | solution.py:442
  13.8 0.0 copy-done
  13.8 5.1 %synth.1 = bf16[16,56,128]{2,1,0:T(8,128)(2,1)S(1)} custom-call(s32[1]{0:T(128)} %bitcast.me, s32[2]{0:T(128)S(1)} %copy-done, bf16[2,2,3,32,32,128]{5,4,3,2,1,0:T(8,128)(2,1)} %get-tuple-element.11.coef_in, bf16[8,2,64,128]{3,2,1,0:T(8,128)(2,1)S(1)} %all-to-all-done.window, bf16[2,2,4096,256]{3,2,1,0:T(8,128)(2,1)} %table.3, ...), custom_call_target="tpu_custom_call" | custom-call | flops 12000000000 | bytes 12000000 | tf_op jit(solution)/shard_map/synth/pallas_call | solution.py:367
  18.9 27.4 %all_to_all.10.got = bf16[16,56,128]{2,1,0:T(8,128)(2,1)S(1)} all-to-all(bf16[16,56,128]{2,1,0:T(8,128)(2,1)S(1)} %synth.1), channel_id=1, replica_groups=mesh['blk'=16,'beam'=8] {'blk'}, dimensions={0} | all-to-all | bytes 458752 | tf_op jit(solution)/shard_map/all_to_all | solution.py:447
  46.2 1.2 %to_map.1 = bf16[16,3,32,128]{3,2,1,0:T(8,128)(2,1)} custom-call(bf16[16,56,128]{2,1,0:T(8,128)(2,1)S(1)} %all_to_all.10.got), custom_call_target="tpu_custom_call" | custom-call | tf_op jit(solution)/shard_map/to_map/pallas_call | solution.py:410
Async XLA Ops:
  1.5 12.3 %all-to-all-start = ((bf16[8,2,64,128]{3,2,1,0:T(8,128)(2,1)}), bf16[8,2,64,128]{3,2,1,0:T(8,128)(2,1)S(1)}, u32[]{:S(2)}, u32[]{:S(2)}) async-start(bf16[8,2,64,128]{3,2,1,0:T(8,128)(2,1)} %broadcast_in_dim.10), calls=%async_computation | async-start | bytes 524288 | tf_op jit(solution)/shard_map/all_to_all | solution.py:442
  7.3 6.5 %copy-start = (s32[2]{0:T(128)S(1)}, s32[2]{0:T(128)}, u32[]{:S(2)}) copy-start(s32[2]{0:T(128)} %modes.1) | copy-start | bytes 28
